TPU v7x, 256 devices: a whole 4x4x8 slice. The times are simulated.
256 devices in a mesh: energy: 128 (over z, y, x), mom: 2 (over core).
Axes of the slice: x: 4, y: 4, z: 8, core: 2. Of those that a mesh axis runs over, the one named last changes fastest.
Arguments:
- lesser: bfloat16 [2, 2, 512, 65536], P('mom', None, 'energy'), may hold values from -6 to 6
- greater: bfloat16 [2, 2, 512, 65536], P('mom', None, 'energy'), may hold values from -6 to 6
- coulomb: bfloat16 [2, 4, 128, 128], P('mom'), may hold values from -0.375 to 0.375
- tile_block: int32 [4], replicated, may hold values from 0 to 3, each once
- shift_table: int32 [2, 2], replicated, may hold values from 0 to 1, each once within a row
Outputs:
- polarization: bfloat16 [2, 2, 512, 65536], P('mom', None, 'energy')
- screened: float32 [2, 2, 128, 65536], P('mom', None, 'energy')
Inputs may be any that keep to these rules, and one draw needn't show every extreme that they name: `tile_block`: each of the 4 tiles holds a different block of the pattern. `shift_table`: each row names every momentum once.
All inputs are finite; a program needn't handle non-finite values.
Results may differ from a plain program's by a relative error of at most 0.0013.
Values may be sent and summed in bfloat16 or wider, within the bound.
A program may use at most 128 MiB of HBM per device.

v0:
```python
import math
import jax
import jax.numpy as jnp
from jax import lax
from jax.sharding import PartitionSpec as P

E = 512


def rotation(product, period, sign):
    angle = 2.0 * math.pi / period * (product % period).astype(jnp.float32)
    return (jnp.cos(angle), sign * jnp.sin(angle))


def complex_einsum(form, table_re, table_im, data_re, data_im, data_axis):
    upper = jnp.concatenate((table_re, -table_im), axis=1)
    lower = jnp.concatenate((table_im, table_re), axis=1)
    table = jnp.concatenate((upper, lower), axis=0)
    data = jnp.concatenate((data_re, data_im), axis=data_axis)
    result = jnp.einsum(
        form, table, data, precision=lax.Precision.HIGH, preferred_element_type=jnp.float32
    )
    half = table_re.shape[0]
    return (result[:half], result[half:])


def transform(data_re, data_im, length, sign):
    radix = 32
    rows, width = data_re.shape
    outer = length // radix
    inner = rows // radix
    shaped_re = data_re.reshape(inner, radix, width)
    shaped_im = data_im.reshape(inner, radix, width)
    freq = jnp.arange(outer, dtype=jnp.int32)
    first_re, first_im = rotation(
        freq[:, None] * jnp.arange(inner, dtype=jnp.int32)[None, :], outer, sign
    )
    mid_re, mid_im = complex_einsum("kn,nmc->kmc", first_re, first_im, shaped_re, shaped_im, 0)
    twist_re, twist_im = rotation(
        freq[:, None] * jnp.arange(radix, dtype=jnp.int32)[None, :], length, sign
    )
    turned_re = mid_re * twist_re[:, :, None] - mid_im * twist_im[:, :, None]
    turned_im = mid_re * twist_im[:, :, None] + mid_im * twist_re[:, :, None]
    digits = jnp.arange(radix, dtype=jnp.int32)
    last_re, last_im = rotation(digits[:, None] * digits[None, :], radix, sign)
    out_re, out_im = complex_einsum("jm,kmc->jkc", last_re, last_im, turned_re, turned_im, 1)
    return (out_re.reshape(length, width), out_im.reshape(length, width))


def spectrum(pair, energies):
    return transform(pair[0].astype(jnp.float32), pair[1].astype(jnp.float32), 2 * energies, -1.0)


def correlate(left, right, rows, energies):
    count = left.shape[0]
    spec_left = [spectrum(left[k], energies) for k in range(count)]
    spec_right = [spectrum(right[k], energies) for k in range(count)]
    right_re = jnp.stack([item[0] for item in spec_right])
    right_im = jnp.stack([item[1] for item in spec_right])
    scale = 1.0 / (math.sqrt(count * energies) * 2 * energies)
    total_re = jnp.zeros_like(spec_left[0][0])
    total_im = jnp.zeros_like(spec_left[0][0])
    for k in range(count):
        other_re = lax.dynamic_index_in_dim(right_re, rows[0, k], 0, keepdims=False)
        other_im = lax.dynamic_index_in_dim(right_im, rows[0, k], 0, keepdims=False)
        total_re = total_re + spec_left[k][0] * other_re + spec_left[k][1] * other_im
        total_im = total_im + spec_left[k][1] * other_re - spec_left[k][0] * other_im
    back_re, back_im = transform(total_re, total_im, 2 * energies, 1.0)
    results = [jnp.stack([-back_im[:energies], back_re[:energies]]) * scale]
    return jnp.stack(results)


def polar_all(left, right, rows, energies):
    columns = left.shape[3]
    width = math.gcd(columns, 128)
    count_q = rows.shape[0]

    def step(index, result):
        start = index * width
        part_left = lax.dynamic_slice_in_dim(left, start, width, 3)
        part_right = lax.dynamic_slice_in_dim(right, start, width, 3)
        block = correlate(part_left, part_right, rows, energies).astype(jnp.bfloat16)
        return lax.dynamic_update_slice_in_dim(result, block, start, 3)

    empty = jnp.zeros((count_q, 2, energies, columns), jnp.bfloat16)
    return lax.fori_loop(0, columns // width, step, empty)


def screen(near, coulomb, tile_block):
    tiles_n = coulomb.shape[1]
    block = coulomb.shape[2]
    band = (tiles_n + 2) // 3
    levels = near.shape[2]
    tiles = near[0].reshape(2, levels, tiles_n, block, block)
    labels = jnp.arange(tiles_n, dtype=jnp.int32)
    onehot = tile_block[:, None] == labels[None, :]
    inverse = jnp.sum(jnp.where(onehot, labels[:, None], 0), axis=0)
    ordered = jnp.take(tiles, inverse, axis=2)
    results = []
    for r in range(band):
        for c in range(max(0, r - 1), min(band, r + 2)):
            acc = jnp.zeros((2, levels, block, block), jnp.float32)
            for l in range(max(0, r - 1), min(band, r + 2)):
                acc = acc + jnp.einsum(
                    "ij,sejk->seik",
                    coulomb[0, 2 * r + l],
                    ordered[:, :, 2 * l + c],
                    preferred_element_type=jnp.float32,
                )
            results.append(acc)
    return jnp.stack(results, axis=2).reshape(1, 2, levels, tiles_n * block * block)


def shards(lesser, greater, coulomb, tile_block, shift_table):
    left, right = (
        lax.all_to_all(lesser, "energy", split_axis=3, concat_axis=2, tiled=True),
        lax.all_to_all(greater, "energy", split_axis=3, concat_axis=2, tiled=True),
    )
    left_all, right_all = (
        lax.all_gather(left, "mom", axis=0, tiled=True),
        lax.all_gather(right, "mom", axis=0, tiled=True),
    )
    rows = lax.dynamic_slice_in_dim(shift_table, lax.axis_index("mom"), 1, 0)
    polar_cols = polar_all(left_all, right_all, rows, E)
    polarization = lax.all_to_all(polar_cols, "energy", split_axis=2, concat_axis=3, tiled=True)
    near = lax.all_to_all(
        polar_cols[:, :, : E // 4], "energy", split_axis=2, concat_axis=3, tiled=True
    )
    return (polarization, screen(near, coulomb, tile_block))


def solution(mesh):
    return jax.shard_map(
        shards,
        mesh=mesh,
        in_specs=(
            P("mom", None, "energy", None),
            P("mom", None, "energy", None),
            P("mom", None, None, None),
            P(),
            P(),
        ),
        out_specs=(P("mom", None, "energy", None), P("mom", None, "energy", None)),
        check_vma=False,
    )
```

profile of v0, /device:TPU:32, one launch (start us, length us, event | category | flops | bytes accessed | tf_op | source)
XLA Modules:
  0.0 771.1 jit_solution(1303767852040457556)
XLA Ops:
  7.2 58.7 %copy.125 = bf16[1,2,4,65536]{2,1,0,3:T(2,128)(2,1)} copy(bf16[1,2,4,65536]{3,2,1,0:T(4,128)(2,1)} %param.7) | data formatting | bytes 2097152 | tf_op args[0]
  65.9 61.1 %reshape.429 = bf16[128,2,2048]{2,1,0:T(2,128)(2,1)S(1)} reshape(bf16[65536,1,2,4]{3,2,1,0:T(2,128)(2,1)} %bitcast.190) | data formatting | bytes 2097152
  127.1 46.2 %all_to_all.63 = bf16[128,2,2048]{2,1,0:T(2,128)(2,1)S(1)} all-to-all(bf16[128,2,2048]{2,1,0:T(2,128)(2,1)S(1)} %reshape.429), channel_id=1, replica_groups=mesh['energy'=128,'mom'=2] {'energy'}, dimensions={0} | all-to-all | bytes 2097152 | tf_op jit(solution)/shard_map/all_to_all | solution.py:116
  173.2 73.1 %reshape.430 = bf16[65536,1,2,4]{3,2,1,0:T(2,128)(2,1)} reshape(bf16[128,2,2048]{2,1,0:T(2,128)(2,1)S(1)} %all_to_all.63) | data formatting | bytes 2097152
  246.3 65.3 %copy.126 = bf16[1,2,128,4,512]{4,3,2,1,0:T(4,128)(2,1)S(1)} copy(bf16[1,2,128,4,512]{3,1,4,2,0:T(2,128)(2,1)} %bitcast.188) | data formatting | bytes 2097152 | tf_op jit(solution)/shard_map/all_to_all | solution.py:116
  312.9 50.9 %copy.127 = bf16[1,2,4,65536]{2,1,0,3:T(2,128)(2,1)} copy(bf16[1,2,4,65536]{3,2,1,0:T(4,128)(2,1)S(1)} %copy-done.2) | data formatting | bytes 2097152 | tf_op args[1]
  363.8 61.1 %reshape.431 = bf16[128,2,2048]{2,1,0:T(2,128)(2,1)S(1)} reshape(bf16[65536,1,2,4]{3,2,1,0:T(2,128)(2,1)} %bitcast.191) | data formatting | bytes 2097152
  424.9 36.4 %all_to_all.64 = bf16[128,2,2048]{2,1,0:T(2,128)(2,1)S(1)} all-to-all(bf16[128,2,2048]{2,1,0:T(2,128)(2,1)S(1)} %reshape.431), channel_id=1, replica_groups=mesh['energy'=128,'mom'=2] {'energy'}, dimensions={0} | all-to-all | bytes 2097152 | tf_op jit(solution)/shard_map/all_to_all | solution.py:117
  461.4 73.1 %reshape.432 = bf16[65536,1,2,4]{3,2,1,0:T(2,128)(2,1)} reshape(bf16[128,2,2048]{2,1,0:T(2,128)(2,1)S(1)} %all_to_all.64) | data formatting | bytes 2097152
  534.5 65.3 %copy.128 = bf16[1,2,128,4,512]{4,3,2,1,0:T(4,128)(2,1)S(1)} copy(bf16[1,2,128,4,512]{3,1,4,2,0:T(2,128)(2,1)} %bitcast.189) | data formatting | bytes 2097152 | tf_op jit(solution)/shard_map/all_to_all | solution.py:117
  605.4 5.2 all-gather.5.cloned.1.call-done
  612.1 82.8 %while.16 = (s32[]{:T(128)}, bf16[1,2,512,512]{3,1,0,2:T(2,128)(2,1)}, bf16[2,2,512,512]{3,2,1,0:T(8,128)(2,1)}, bf16[2,2,512,512]{3,2,1,0:T(8,128)(2,1)}, s32[]...) while((s32[]{:T(128)}, bf16[1,2,512,512]{3,1,0,2:T(2,128)(2,1)}, ...), condition=%wide.region_1.2_spmd, body=%wide.region_0.1_spmd.sunk | while | flops 815953408 | bytes 64403652 | solution.py:86
  616.8 1.5 fusion.159
  618.7 2.0 multiply_subtract_fusion.8
  637.5 1.5 fusion.159
  639.4 2.0 multiply_subtract_fusion.8
  660.1 2.0 multiply_subtract_fusion.8
  680.7 2.0 multiply_subtract_fusion.8
  694.9 1.8 slice.403
  696.7 13.7 %all-to-all-start.3 = ((bf16[1,2,128,512]{3,1,0,2:T(2,128)(2,1)}), bf16[1,2,128,512]{3,1,0,2:T(2,128)(2,1)S(1)}, u32[]{:S(2)}, u32[]{:S(2)}) async-start(bf16[1,2,128,512]{3,1,0,2:T(2,128)(2,1)} %slice.403), calls=%async_computation.3 | async-start | bytes 524288 | tf_op jit(solution)/shard_map/all_to_all | solution.py:126
  710.6 15.1 %all-to-all-done.3 = bf16[1,2,128,512]{3,1,0,2:T(2,128)(2,1)S(1)} async-done(((bf16[1,2,128,512]{3,1,0,2:T(2,128)(2,1)}), bf16[1,2,128,512]{3,1,0,2:T(2,128)(2,1)S(1)}, u32[]{:S(2)}, u32[]{:S(2)}) %all-to-all-start.3) | async-done | bytes 262176 | tf_op jit(solution)/shard_map/all_to_all | solution.py:126
  725.7 6.5 all-to-all-start.2
  735.8 26.6 %all-to-all-done.2 = bf16[1,2,512,512]{3,1,0,2:T(2,128)(2,1)S(1)} async-done(((bf16[1,2,512,512]{3,1,0,2:T(2,128)(2,1)}), bf16[1,2,512,512]{3,1,0,2:T(2,128)(2,1)S(1)}, u32[]{:S(2)}, u32[]{:S(2)}) %all-to-all-start.2) | async-done | bytes 1048608 | tf_op jit(solution)/shard_map/all_to_all | solution.py:125
  762.7 1.6 all_to_all.57
  (242 shorter events, 78.7 us)
Async XLA Ops:
  7.2 593.8 %copy-start = (s32[2,2]{1,0:T(2,128)S(1)}, s32[2,2]{1,0:T(2,128)}, u32[]{:S(2)}) copy-start(s32[2,2]{1,0:T(2,128)} %param.11) | copy-start | bytes 52
  7.2 598.2 %all-gather.3.cloned.1.call-start = ((), (), s32[]{:S(2)}) async-start(), calls=%async_computation.4 | async-start | bytes 3145728 | tf_op jit(solution)/shard_map/all_gather | solution.py:120
  173.2 139.6 %copy-start.2 = (bf16[1,2,4,65536]{3,2,1,0:T(4,128)(2,1)S(1)}, bf16[1,2,4,65536]{3,2,1,0:T(4,128)(2,1)}, u32[]{:S(2)}) copy-start(bf16[1,2,4,65536]{3,2,1,0:T(4,128)(2,1)} %param.8) | copy-start | bytes 3145732
  312.8 297.8 %all-gather.5.cloned.1.call-start = ((), (), s32[]{:S(2)}) async-start(), calls=%async_computation.5 | async-start | bytes 3145728 | tf_op jit(solution)/shard_map/all_gather | solution.py:121
  612.1 98.3 %copy-start.4 = (s32[4]{0:T(128)S(1)}, s32[4]{0:T(128)}, u32[]{:S(2)}) copy-start(s32[4]{0:T(128)} %param.10) | copy-start | bytes 52
  612.1 121.3 %copy-start.3 = (bf16[1,4,128,128]{3,2,1,0:T(8,128)(2,1)S(1)}, bf16[1,4,128,128]{3,2,1,0:T(8,128)(2,1)}, u32[]{:S(2)}) copy-start(bf16[1,4,128,128]{3,2,1,0:T(8,128)(2,1)} %param.9) | copy-start | bytes 393220
  694.9 69.4 %copy-start.1 = (s32[2,2]{1,0:T(2,128)S(1)}, s32[2,2]{1,0:T(2,128)}, u32[]{:S(2)}) copy-start(s32[2,2]{1,0:T(2,128)} %param.11) | copy-start | bytes 52
  696.7 28.9 %all-to-all-start.3 = ((bf16[1,2,128,512]{3,1,0,2:T(2,128)(2,1)}), bf16[1,2,128,512]{3,1,0,2:T(2,128)(2,1)S(1)}, u32[]{:S(2)}, u32[]{:S(2)}) async-start(bf16[1,2,128,512]{3,1,0,2:T(2,128)(2,1)} %slice.403), calls=%async_computation.3 | async-start | bytes 524288 | tf_op jit(solution)/shard_map/all_to_all | solution.py:126
  725.7 36.7 %all-to-all-start.2 = ((bf16[1,2,512,512]{3,1,0,2:T(2,128)(2,1)}), bf16[1,2,512,512]{3,1,0,2:T(2,128)(2,1)S(1)}, u32[]{:S(2)}, u32[]{:S(2)}) async-start(bf16[1,2,512,512]{3,1,0,2:T(2,128)(2,1)} %get-tuple-element.179), calls=%async_computation.2 | async-start | bytes 2097152 | tf_op jit(solution)/shard_map/all_to_all | solution.py:125
Sparse Core Ops, SparseCore 0:
  312.9 9.4 all-gather.2
  601.1 9.4 all-gather.4
where the time goes:
time: 779 us; the launch traced here: 771 us
  local copies, waits for them, and re-layouts  541 us (69%)
  blocking collectives  82.6 us (11%)
  waiting for transfers between devices  47 us (6%)
  matrix products  39.7 us (5%)
  other arithmetic  21.5 us (3%)
  starting transfers between devices  20.3 us (3%)
  between operations  18 us (2%)
    unnamed x16, local copies, waits for them, and re-layouts  378 us
    all_to_all x2, local copies, waits for them, and re-layouts, shards(): lax.all_to_all(greater, 'energy', split_axis=3, concat_axis=2, tiled=True)  66.5 us
    all_to_all x2, local copies, waits for them, and re-layouts, shards(): lax.all_to_all(lesser, 'energy', split_axis=3, concat_axis=2, tiled=True)  66.4 us
    all_to_all x1, blocking collectives, shards(): lax.all_to_all(lesser, 'energy', split_axis=3, concat_axis=2, tiled=True)  46.2 us
    dot_general x40, matrix products, complex_einsum(): jnp.einsum(form, table, data, precision=lax.Precision.HIGH, preferred_ele...  38.4 us
    all_to_all x1, blocking collectives, shards(): lax.all_to_all(greater, 'energy', split_axis=3, concat_axis=2, tiled=True)  36.4 us
    all_to_all x1, waiting for transfers between devices, shards(): lax.all_to_all(polar_cols, 'energy', split_axis=2, concat_axis=3, tiled=T...  26.6 us
  transfers between devices with their start and end apart: 4, of which 3 were waited for; matrix products, arithmetic and copies ran while one was open for 33% of the time, Pallas kernels for 0%

commit v1 on v0

--- a/solution.py
+++ b/solution.py
@@ -113,7 +113,12 @@
 
 def shards(lesser, greater, coulomb, tile_block, shift_table):
     left, right = (
-        lax.all_to_all(lesser, "energy", split_axis=3, concat_axis=2, tiled=True),
+        jnp.concatenate(
+            lax.all_to_all(
+                jnp.stack(jnp.split(lesser, lax.axis_size("energy"), axis=3)), "energy", 0, 0
+            ),
+            axis=2,
+        ),
         lax.all_to_all(greater, "energy", split_axis=3, concat_axis=2, tiled=True),
     )
     left_all, right_all = (

time: 779 us -> 612 us (0.79)
  local copies, waits for them, and re-layouts: 541 us -> 374 us
    unnamed x16 -> x140, local copies, waits for them, and re-layouts: 378 us -> 275 us
    all_to_all x2 -> x0, local copies, waits for them, and re-layouts: 66.4 us -> none  [shards(): lax.all_to_all(lesser, 'energy', split_axis=3, concat_axis=2, tiled=True)]
  transfers between devices with their start and end apart: 4 -> 4, of which waited for: 3 -> 3; matrix products, arithmetic and copies ran while one was open for 33% -> 42% of each run, Pallas kernels for 0% -> 0%
where the time goes in v1:
time: 612 us; the launch traced here: 604 us
  local copies, waits for them, and re-layouts  374 us (61%)
  blocking collectives  82.6 us (13%)
  waiting for transfers between devices  47 us (8%)
  matrix products  39.8 us (7%)
  other arithmetic  21.5 us (4%)
  starting transfers between devices  20.3 us (3%)
  between operations  18.1 us (3%)
    unnamed x140, local copies, waits for them, and re-layouts  275 us
    all_to_all x2, local copies, waits for them, and re-layouts, shards(): lax.all_to_all(greater, 'energy', split_axis=3, concat_axis=2, tiled=True)  66.5 us
    all_to_all x1, blocking collectives, shards(): lax.all_to_all(jnp.stack(jnp.split(lesser, lax.axis_size('energy'), axis=...  46.1 us
    dot_general x40, matrix products, complex_einsum(): jnp.einsum(form, table, data, precision=lax.Precision.HIGH, preferred_ele...  38.5 us
    all_to_all x1, blocking collectives, shards(): lax.all_to_all(greater, 'energy', split_axis=3, concat_axis=2, tiled=True)  36.4 us
    all_to_all x1, waiting for transfers between devices, shards(): lax.all_to_all(polar_cols, 'energy', split_axis=2, concat_axis=3, tiled=T...  26.6 us
    all_to_all x1, waiting for transfers between devices, shards(): lax.all_to_all(polar_cols[:, :, :E // 4], 'energy', split_axis=2, concat_...  15.1 us
    all_to_all x1, starting transfers between devices, shards(): lax.all_to_all(polar_cols[:, :, :E // 4], 'energy', split_axis=2, concat_...  13.7 us
  transfers between devices with their start and end apart: 4, of which 3 were waited for; matrix products, arithmetic and copies ran while one was open for 42% of the time, Pallas kernels for 0%

profile of v1, /device:TPU:32, one launch (start us, length us, event | category | flops | bytes accessed | tf_op | source)
XLA Modules:
  0.0 604.3 jit_solution(5182563067995911619)
XLA Ops:
  98.0 46.1 %all_to_all.50 = bf16[128,1,2,4,512]{4,3,2,1,0:T(4,128)(2,1)S(1)} all-to-all(bf16[128,1,2,4,512]{4,3,2,1,0:T(4,128)(2,1)S(1)} %constant_dynamic-update-slice_fusion), channel_id=1, replica_groups=mesh['energy'=128,'mom'=2] {'energy'}, dimensions={0} | all-to-all | bytes 2097152 | tf_op jit(solution)/shard_map/all_to_all | solution.py:117
  146.1 50.8 %copy.125 = bf16[1,2,4,65536]{2,1,0,3:T(2,128)(2,1)} copy(bf16[1,2,4,65536]{3,2,1,0:T(4,128)(2,1)S(1)} %copy-done.2) | data formatting | bytes 2097152 | tf_op args[1]
  196.9 61.1 %reshape.437 = bf16[128,2,2048]{2,1,0:T(2,128)(2,1)S(1)} reshape(bf16[65536,1,2,4]{3,2,1,0:T(2,128)(2,1)} %bitcast.441) | data formatting | bytes 2097152
  258.0 36.4 %all_to_all.51 = bf16[128,2,2048]{2,1,0:T(2,128)(2,1)S(1)} all-to-all(bf16[128,2,2048]{2,1,0:T(2,128)(2,1)S(1)} %reshape.437), channel_id=1, replica_groups=mesh['energy'=128,'mom'=2] {'energy'}, dimensions={0} | all-to-all | bytes 2097152 | tf_op jit(solution)/shard_map/all_to_all | solution.py:122
  294.5 73.1 %reshape.438 = bf16[65536,1,2,4]{3,2,1,0:T(2,128)(2,1)} reshape(bf16[128,2,2048]{2,1,0:T(2,128)(2,1)S(1)} %all_to_all.51) | data formatting | bytes 2097152
  367.6 65.3 %copy.126 = bf16[1,2,128,4,512]{4,3,2,1,0:T(4,128)(2,1)S(1)} copy(bf16[1,2,128,4,512]{3,1,4,2,0:T(2,128)(2,1)} %bitcast.440) | data formatting | bytes 2097152 | tf_op jit(solution)/shard_map/all_to_all | solution.py:122
  438.5 5.2 all-gather.5.cloned.1.call-done
  443.7 1.5 broadcast_in_dim.29.clone
  445.2 82.8 %while.16 = (s32[]{:T(128)}, bf16[1,2,512,512]{3,1,0,2:T(2,128)(2,1)}, bf16[2,2,512,512]{3,2,1,0:T(8,128)(2,1)}, bf16[2,2,512,512]{3,2,1,0:T(8,128)(2,1)}, s32[]...) while((s32[]{:T(128)}, bf16[1,2,512,512]{3,1,0,2:T(2,128)(2,1)}, ...), condition=%wide.region_1.2_spmd, body=%wide.region_0.1_spmd.sunk | while | flops 815953408 | bytes 64403652 | solution.py:86
  449.9 1.5 fusion.159
  451.8 2.0 multiply_subtract_fusion.8
  460.9 1.3 multiply_add_fusion.7
  470.6 1.5 fusion.159
  472.5 2.0 multiply_subtract_fusion.8
  491.3 1.5 fusion.159
  493.2 2.0 multiply_subtract_fusion.8
  512.0 1.5 fusion.159
  513.9 2.0 multiply_subtract_fusion.8
  528.1 1.8 slice.403
  529.9 13.7 %all-to-all-start.3 = ((bf16[1,2,128,512]{3,1,0,2:T(2,128)(2,1)}), bf16[1,2,128,512]{3,1,0,2:T(2,128)(2,1)S(1)}, u32[]{:S(2)}, u32[]{:S(2)}) async-start(bf16[1,2,128,512]{3,1,0,2:T(2,128)(2,1)} %slice.403), calls=%async_computation.3 | async-start | bytes 524288 | tf_op jit(solution)/shard_map/all_to_all | solution.py:131
  543.7 15.1 %all-to-all-done.3 = bf16[1,2,128,512]{3,1,0,2:T(2,128)(2,1)S(1)} async-done(((bf16[1,2,128,512]{3,1,0,2:T(2,128)(2,1)}), bf16[1,2,128,512]{3,1,0,2:T(2,128)(2,1)S(1)}, u32[]{:S(2)}, u32[]{:S(2)}) %all-to-all-start.3) | async-done | bytes 262176 | tf_op jit(solution)/shard_map/all_to_all | solution.py:131
  558.8 6.5 %all-to-all-start.2 = ((bf16[1,2,512,512]{3,1,0,2:T(2,128)(2,1)}), bf16[1,2,512,512]{3,1,0,2:T(2,128)(2,1)S(1)}, u32[]{:S(2)}, u32[]{:S(2)}) async-start(bf16[1,2,512,512]{3,1,0,2:T(2,128)(2,1)} %get-tuple-element.179), calls=%async_computation.2 | async-start | bytes 2097152 | tf_op jit(solution)/shard_map/all_to_all | solution.py:130
  568.9 26.6 %all-to-all-done.2 = bf16[1,2,512,512]{3,1,0,2:T(2,128)(2,1)S(1)} async-done(((bf16[1,2,512,512]{3,1,0,2:T(2,128)(2,1)}), bf16[1,2,512,512]{3,1,0,2:T(2,128)(2,1)S(1)}, u32[]{:S(2)}, u32[]{:S(2)}) %all-to-all-start.2) | async-done | bytes 1048608 | tf_op jit(solution)/shard_map/all_to_all | solution.py:130
  595.8 1.6 all_to_all.44
  (367 shorter events, 164.4 us)
Async XLA Ops:
  7.2 426.9 %copy-start = (s32[2,2]{1,0:T(2,128)S(1)}, s32[2,2]{1,0:T(2,128)}, u32[]{:S(2)}) copy-start(s32[2,2]{1,0:T(2,128)} %param.11) | copy-start | bytes 52
  7.2 431.3 %all-gather.3.cloned.1.call-start = ((), (), s32[]{:S(2)}) async-start(), calls=%async_computation.4 | async-start | bytes 3145728 | tf_op jit(solution)/shard_map/all_gather | solution.py:125
  144.5 1.6 copy-start.2
  145.7 298.1 %all-gather.5.cloned.1.call-start = ((), (), s32[]{:S(2)}) async-start(), calls=%async_computation.5 | async-start | bytes 3145728 | tf_op jit(solution)/shard_map/all_gather | solution.py:126
  445.2 98.3 %copy-start.4 = (s32[4]{0:T(128)S(1)}, s32[4]{0:T(128)}, u32[]{:S(2)}) copy-start(s32[4]{0:T(128)} %param.10) | copy-start | bytes 52
  529.9 28.9 %all-to-all-start.3 = ((bf16[1,2,128,512]{3,1,0,2:T(2,128)(2,1)}), bf16[1,2,128,512]{3,1,0,2:T(2,128)(2,1)S(1)}, u32[]{:S(2)}, u32[]{:S(2)}) async-start(bf16[1,2,128,512]{3,1,0,2:T(2,128)(2,1)} %slice.403), calls=%async_computation.3 | async-start | bytes 524288 | tf_op jit(solution)/shard_map/all_to_all | solution.py:131
  543.7 22.8 %copy-start.3 = (bf16[1,4,128,128]{3,2,1,0:T(8,128)(2,1)S(1)}, bf16[1,4,128,128]{3,2,1,0:T(8,128)(2,1)}, u32[]{:S(2)}) copy-start(bf16[1,4,128,128]{3,2,1,0:T(8,128)(2,1)} %param.9) | copy-start | bytes 393220
  558.8 36.7 %all-to-all-start.2 = ((bf16[1,2,512,512]{3,1,0,2:T(2,128)(2,1)}), bf16[1,2,512,512]{3,1,0,2:T(2,128)(2,1)S(1)}, u32[]{:S(2)}, u32[]{:S(2)}) async-start(bf16[1,2,512,512]{3,1,0,2:T(2,128)(2,1)} %get-tuple-element.179), calls=%async_computation.2 | async-start | bytes 2097152 | tf_op jit(solution)/shard_map/all_to_all | solution.py:130
  595.5 1.9 copy-start.1
Sparse Core Ops, SparseCore 0:
  145.8 9.4 all-gather.2
  434.2 9.4 all-gather.4
